TPU v7x, 32 devices: a whole 2x2x4 slice. The times are simulated.
32 devices in a mesh: rep: 4 (over x, core), fsdp: 8 (over z, y).
Axes of the slice: x: 2, y: 2, z: 4, core: 2. Of those that a mesh axis runs over, the one named last changes fastest.
Arguments:
- layer_input: bfloat16 [24576, 1024], P(('rep', 'fsdp')), may hold values from -6 to 6
- item_ids: int32 [24576], P(('rep', 'fsdp')), may hold values from 0 to 48, as said below
- norm_gain: bfloat16 [1024], P('fsdp'), may hold values from 0.25 to 1.75
- norm_bias: bfloat16 [1024], P('fsdp'), may hold values from -1.5 to 1.5
- joint_weight: bfloat16 [1024, 3072], P('fsdp'), may hold values from -0.1875 to 0.1875
- joint_bias: bfloat16 [2048], P('fsdp'), may hold values from -1.5 to 1.5
- out_weight: bfloat16 [1024, 1024], P('fsdp'), may hold values from -0.5 to 0.5
- out_bias: bfloat16 [1024], P('fsdp'), may hold values from -1.5 to 1.5
- second_gain: bfloat16 [1024], P('fsdp'), may hold values from 0.25 to 1.75
- second_bias: bfloat16 [1024], P('fsdp'), may hold values from -1.5 to 1.5
- up_weight: bfloat16 [1024, 2048], P('fsdp'), may hold values from -0.1875 to 0.1875
- up_bias: bfloat16 [2048], P('fsdp'), may hold values from -1.5 to 1.5
- down_weight: bfloat16 [2048, 1024], P('fsdp'), may hold values from -0.125 to 0.125
- down_bias: bfloat16 [1024], P('fsdp'), may hold values from -1.5 to 1.5
- output_grad: bfloat16 [24576, 1024], P(('rep', 'fsdp')), may hold values from -6 to 6
Outputs:
- layer_output: bfloat16 [24576, 1024], P(('rep', 'fsdp'))
- input_grad: bfloat16 [24576, 1024], P(('rep', 'fsdp'))
- norm_gain_grad: float32 [1024], P('fsdp')
- norm_bias_grad: float32 [1024], P('fsdp')
- joint_weight_grad: float32 [1024, 3072], P('fsdp')
- joint_bias_grad: float32 [2048], P('fsdp')
- out_weight_grad: float32 [1024, 1024], P('fsdp')
- out_bias_grad: float32 [1024], P('fsdp')
- second_gain_grad: float32 [1024], P('fsdp')
- second_bias_grad: float32 [1024], P('fsdp')
- up_weight_grad: float32 [1024, 2048], P('fsdp')
- up_bias_grad: float32 [2048], P('fsdp')
- down_weight_grad: float32 [2048, 1024], P('fsdp')
- down_bias_grad: float32 [1024], P('fsdp')
Inputs may be any that keep to these rules, and one draw needn't show every extreme that they name: `item_ids`: every aligned block of 768 rows holds whole items, numbered 0, 1, 2, ... in order of position inside the block; items have 15 or 60 tokens, save at most one item of fewer than 15 tokens in a block, and each block holds at least one item of 60 tokens.
All inputs are finite; a program needn't handle non-finite values.
Results may differ from a plain program's by a relative error of at most 0.018.
Values may be sent and summed in bfloat16 or wider, within the bound.
No kernel may reach another device: no remote copies, remote signals or barrier semaphores. Data moves between devices by JAX's collectives and lax.ppermute only.
A program may use at most 192 MiB of HBM per device.

v0:
```python
import jax
import jax.numpy as jnp
from jax import lax
from jax.sharding import PartitionSpec as P

H = 8
HD = 128
QBLK = 768
eps = 1e-05
masked_score = -1e30


def norm_affine(values, gain, bias):
    center = values - jnp.mean(values, axis=-1, keepdims=True)
    spread = jnp.mean(center * center, axis=-1, keepdims=True)
    return center * lax.rsqrt(spread + eps) * gain + bias


def split_heads(matrix):
    blocks = matrix.shape[0] // QBLK
    return matrix.reshape(blocks, QBLK, H, HD).transpose(0, 2, 1, 3).reshape(blocks * H, QBLK, HD)


def merge_heads(stacked):
    blocks = stacked.shape[0] // H
    return stacked.reshape(blocks, H, QBLK, HD).transpose(0, 2, 1, 3).reshape(blocks * QBLK, H * HD)


def block_scores(queries, key_rows, labels):
    scores = lax.dot_general(
        queries, key_rows, (((1,), (1,)), ((), ())), preferred_element_type=jnp.float32
    ) * HD ** (-0.5)
    position = jnp.arange(QBLK)
    allowed = (labels[:, None] == labels[None, :]) & (position[:, None] >= position[None, :])
    return jnp.where(allowed, scores, masked_score)


def head_forward(pieces):
    queries, key_rows, value_rows, labels = pieces
    scores = block_scores(queries, key_rows, labels)
    peak = jnp.max(scores, axis=1, keepdims=True)
    raised = jnp.exp(scores - peak)
    partition = jnp.sum(raised, axis=1, keepdims=True)
    weights = (raised / partition).astype(jnp.bfloat16)
    mixed = jnp.dot(weights, value_rows, preferred_element_type=jnp.float32).astype(jnp.bfloat16)
    return (mixed, (peak + jnp.log(partition))[:, 0])


def head_backward(pieces):
    queries, key_rows, value_rows, labels, upstream, logsum = pieces
    weights = jnp.exp(block_scores(queries, key_rows, labels) - logsum[:, None])
    dweights = lax.dot_general(
        upstream, value_rows, (((1,), (1,)), ((), ())), preferred_element_type=jnp.float32
    )
    grad_value = lax.dot_general(
        weights.astype(jnp.bfloat16),
        upstream,
        (((0,), (0,)), ((), ())),
        preferred_element_type=jnp.float32,
    )
    inner = jnp.sum(weights * dweights, axis=1, keepdims=True)
    dscores = (weights * (dweights - inner)).astype(jnp.bfloat16)
    grad_query = jnp.dot(dscores, key_rows, preferred_element_type=jnp.float32) * HD ** (-0.5)
    grad_key = lax.dot_general(
        dscores, queries, (((0,), (0,)), ((), ())), preferred_element_type=jnp.float32
    ) * HD ** (-0.5)
    return (grad_query, grad_key, grad_value)


def transposed_dot(left, right):
    return lax.dot_general(
        left, right, (((0,), (0,)), ((), ())), preferred_element_type=jnp.float32
    )


def dot_transposed(left, right):
    return lax.dot_general(
        left, right, (((1,), (1,)), ((), ())), preferred_element_type=jnp.float32
    )


def on_device(
    layer_input,
    item_ids,
    norm_gain,
    norm_bias,
    joint_weight,
    joint_bias,
    out_weight,
    out_bias,
    second_gain,
    second_bias,
    up_weight,
    up_bias,
    down_weight,
    down_bias,
    output_grad,
):
    width = layer_input.shape[1]
    row_count = layer_input.shape[0]
    blocks = row_count // QBLK
    gain_one, bias_one, joint_full, joint_shift, out_full, out_shift = (
        lax.all_gather(norm_gain, "fsdp", axis=0, tiled=True),
        lax.all_gather(norm_bias, "fsdp", axis=0, tiled=True),
        lax.all_gather(joint_weight, "fsdp", axis=0, tiled=True),
        lax.all_gather(joint_bias, "fsdp", axis=0, tiled=True),
        lax.all_gather(out_weight, "fsdp", axis=0, tiled=True),
        lax.all_gather(out_bias, "fsdp", axis=0, tiled=True),
    )
    inputs = layer_input.astype(jnp.float32)
    bias_one_f = bias_one.astype(jnp.float32)
    first = norm_affine(inputs, gain_one.astype(jnp.float32), bias_one_f).astype(jnp.bfloat16)
    projected = jnp.dot(first, joint_full, preferred_element_type=jnp.float32)
    shift_f = joint_shift.astype(jnp.float32)
    queries = (projected[:, :width] + shift_f[:width]).astype(jnp.bfloat16)
    key_rows = projected[:, width : 2 * width].astype(jnp.bfloat16)
    value_rows = (projected[:, 2 * width :] + shift_f[width:]).astype(jnp.bfloat16)
    head_queries = split_heads(queries)
    head_keys = split_heads(key_rows)
    head_values = split_heads(value_rows)
    head_labels = jnp.broadcast_to(item_ids.reshape(blocks, 1, QBLK), (blocks, H, QBLK)).reshape(
        blocks * H, QBLK
    )
    head_mixed, logsum = lax.map(head_forward, (head_queries, head_keys, head_values, head_labels))
    attended = merge_heads(head_mixed)
    middle = (
        inputs
        + jnp.dot(attended, out_full, preferred_element_type=jnp.float32)
        + out_shift.astype(jnp.float32)
    )
    gain_two, bias_two, up_full, up_shift, down_full, down_shift = (
        lax.all_gather(second_gain, "fsdp", axis=0, tiled=True),
        lax.all_gather(second_bias, "fsdp", axis=0, tiled=True),
        lax.all_gather(up_weight, "fsdp", axis=0, tiled=True),
        lax.all_gather(up_bias, "fsdp", axis=0, tiled=True),
        lax.all_gather(down_weight, "fsdp", axis=0, tiled=True),
        lax.all_gather(down_bias, "fsdp", axis=0, tiled=True),
    )
    bias_two_f = bias_two.astype(jnp.float32)
    second = norm_affine(middle, gain_two.astype(jnp.float32), bias_two_f).astype(jnp.bfloat16)
    hidden = jnp.dot(second, up_full, preferred_element_type=jnp.float32) + up_shift.astype(
        jnp.float32
    )
    active = jax.nn.gelu(hidden).astype(jnp.bfloat16)
    feed_out = jnp.dot(active, down_full, preferred_element_type=jnp.float32) + down_shift.astype(
        jnp.float32
    )
    layer_output = (middle + feed_out).astype(jnp.bfloat16)
    gain_two_back, up_back, down_back = (
        lax.all_gather(second_gain, "fsdp", axis=0, tiled=True),
        lax.all_gather(up_weight, "fsdp", axis=0, tiled=True),
        lax.all_gather(down_weight, "fsdp", axis=0, tiled=True),
    )
    upstream = output_grad.astype(jnp.float32)
    grad_down = transposed_dot(active, output_grad)
    grad_down_shift = jnp.sum(upstream, axis=0)
    dactive = dot_transposed(output_grad, down_back)
    gelu_value, gelu_pull = jax.vjp(jax.nn.gelu, hidden)
    dhidden = gelu_pull(dactive)[0].astype(jnp.bfloat16)
    grad_up = transposed_dot(second, dhidden)
    grad_up_shift = jnp.sum(dhidden.astype(jnp.float32), axis=0)
    dsecond = dot_transposed(dhidden, up_back)
    norm_value, second_pull = jax.vjp(
        norm_affine, middle, gain_two_back.astype(jnp.float32), bias_two_f
    )
    dmiddle_part, grad_gain_two, grad_bias_two = second_pull(dsecond)
    dmiddle = upstream + dmiddle_part
    grad_gain_two, grad_bias_two, grad_up, grad_up_shift, grad_down, grad_down_shift = (
        lax.psum_scatter(
            grad_gain_two.astype(jnp.bfloat16), "fsdp", scatter_dimension=0, tiled=True
        ).astype(jnp.float32),
        lax.psum_scatter(
            grad_bias_two.astype(jnp.bfloat16), "fsdp", scatter_dimension=0, tiled=True
        ).astype(jnp.float32),
        lax.psum_scatter(
            grad_up.astype(jnp.bfloat16), "fsdp", scatter_dimension=0, tiled=True
        ).astype(jnp.float32),
        lax.psum_scatter(
            grad_up_shift.astype(jnp.bfloat16), "fsdp", scatter_dimension=0, tiled=True
        ).astype(jnp.float32),
        lax.psum_scatter(
            grad_down.astype(jnp.bfloat16), "fsdp", scatter_dimension=0, tiled=True
        ).astype(jnp.float32),
        lax.psum_scatter(
            grad_down_shift.astype(jnp.bfloat16), "fsdp", scatter_dimension=0, tiled=True
        ).astype(jnp.float32),
    )
    gain_one_back, joint_back, out_back = (
        lax.all_gather(norm_gain, "fsdp", axis=0, tiled=True),
        lax.all_gather(joint_weight, "fsdp", axis=0, tiled=True),
        lax.all_gather(out_weight, "fsdp", axis=0, tiled=True),
    )
    dbranch = dmiddle.astype(jnp.bfloat16)
    grad_out = transposed_dot(attended, dbranch)
    grad_out_shift = jnp.sum(dbranch.astype(jnp.float32), axis=0)
    dattended = dot_transposed(dbranch, out_back).astype(jnp.bfloat16)
    grad_queries, grad_keys, grad_values = lax.map(
        head_backward,
        (head_queries, head_keys, head_values, head_labels, split_heads(dattended), logsum),
    )
    dprojected = jnp.concatenate(
        [merge_heads(grad_queries), merge_heads(grad_keys), merge_heads(grad_values)], axis=1
    ).astype(jnp.bfloat16)
    grad_joint = transposed_dot(first, dprojected)
    dprojected_f = dprojected.astype(jnp.float32)
    grad_joint_shift = jnp.concatenate(
        [jnp.sum(dprojected_f[:, :width], axis=0), jnp.sum(dprojected_f[:, 2 * width :], axis=0)]
    )
    dfirst = dot_transposed(dprojected, joint_back)
    first_value, first_pull = jax.vjp(
        norm_affine, inputs, gain_one_back.astype(jnp.float32), bias_one_f
    )
    dinput_part, grad_gain_one, grad_bias_one = first_pull(dfirst)
    input_grad = (dmiddle + dinput_part).astype(jnp.bfloat16)
    grad_gain_one, grad_bias_one, grad_joint, grad_joint_shift, grad_out, grad_out_shift = (
        lax.psum_scatter(
            grad_gain_one.astype(jnp.bfloat16), "fsdp", scatter_dimension=0, tiled=True
        ).astype(jnp.float32),
        lax.psum_scatter(
            grad_bias_one.astype(jnp.bfloat16), "fsdp", scatter_dimension=0, tiled=True
        ).astype(jnp.float32),
        lax.psum_scatter(
            grad_joint.astype(jnp.bfloat16), "fsdp", scatter_dimension=0, tiled=True
        ).astype(jnp.float32),
        lax.psum_scatter(
            grad_joint_shift.astype(jnp.bfloat16), "fsdp", scatter_dimension=0, tiled=True
        ).astype(jnp.float32),
        lax.psum_scatter(
            grad_out.astype(jnp.bfloat16), "fsdp", scatter_dimension=0, tiled=True
        ).astype(jnp.float32),
        lax.psum_scatter(
            grad_out_shift.astype(jnp.bfloat16), "fsdp", scatter_dimension=0, tiled=True
        ).astype(jnp.float32),
    )
    (
        grad_gain_one,
        grad_bias_one,
        grad_joint,
        grad_joint_shift,
        grad_out,
        grad_out_shift,
        grad_gain_two,
        grad_bias_two,
        grad_up,
        grad_up_shift,
        grad_down,
        grad_down_shift,
    ) = (
        lax.psum(grad_gain_one.astype(jnp.bfloat16), "rep").astype(jnp.float32),
        lax.psum(grad_bias_one.astype(jnp.bfloat16), "rep").astype(jnp.float32),
        lax.psum(grad_joint.astype(jnp.bfloat16), "rep").astype(jnp.float32),
        lax.psum(grad_joint_shift.astype(jnp.bfloat16), "rep").astype(jnp.float32),
        lax.psum(grad_out.astype(jnp.bfloat16), "rep").astype(jnp.float32),
        lax.psum(grad_out_shift.astype(jnp.bfloat16), "rep").astype(jnp.float32),
        lax.psum(grad_gain_two.astype(jnp.bfloat16), "rep").astype(jnp.float32),
        lax.psum(grad_bias_two.astype(jnp.bfloat16), "rep").astype(jnp.float32),
        lax.psum(grad_up.astype(jnp.bfloat16), "rep").astype(jnp.float32),
        lax.psum(grad_up_shift.astype(jnp.bfloat16), "rep").astype(jnp.float32),
        lax.psum(grad_down.astype(jnp.bfloat16), "rep").astype(jnp.float32),
        lax.psum(grad_down_shift.astype(jnp.bfloat16), "rep").astype(jnp.float32),
    )
    return (
        layer_output,
        input_grad,
        grad_gain_one,
        grad_bias_one,
        grad_joint,
        grad_joint_shift,
        grad_out,
        grad_out_shift,
        grad_gain_two,
        grad_bias_two,
        grad_up,
        grad_up_shift,
        grad_down,
        grad_down_shift,
    )


def solution(mesh):
    placed = (
        P(("rep", "fsdp"), None),
        P(("rep", "fsdp")),
        P("fsdp"),
        P("fsdp"),
        P("fsdp", None),
        P("fsdp"),
        P("fsdp", None),
        P("fsdp"),
        P("fsdp"),
        P("fsdp"),
        P("fsdp", None),
        P("fsdp"),
        P("fsdp", None),
        P("fsdp"),
        P(("rep", "fsdp"), None),
    )
    return jax.shard_map(
        on_device,
        mesh=mesh,
        in_specs=placed,
        out_specs=(
            P(("rep", "fsdp"), None),
            P(("rep", "fsdp"), None),
            P("fsdp"),
            P("fsdp"),
            P("fsdp", None),
            P("fsdp"),
            P("fsdp", None),
            P("fsdp"),
            P("fsdp"),
            P("fsdp"),
            P("fsdp", None),
            P("fsdp"),
            P("fsdp", None),
            P("fsdp"),
        ),
        check_vma=False,
    )
```

profile of v0, /device:TPU:0, one launch (start us, length us, event | category | flops | bytes accessed | tf_op | source)
XLA Modules:
  0.0 769.2 jit_solution(3482385792619113970)
XLA Ops:
  11.4 22.8 %all-gather = bf16[8,1,128]{2,1,0:T(2,128)(2,1)S(1)} all-gather(bf16[1,1,128]{2,1,0:T(2,128)(2,1)} %bitcast.201), channel_id=1, replica_groups=mesh['rep'=4,'fsdp'=8] {'fsdp'}, dimensions={0}, use_global_device_ids=true | all-gather | bytes 2304 | tf_op jit(solution)/shard_map/all_gather | solution.py:103
  34.2 17.2 %all-gather.1 = bf16[8,1,128]{2,1,0:T(2,128)(2,1)S(1)} all-gather(bf16[1,1,128]{2,1,0:T(2,128)(2,1)} %bitcast.202), channel_id=1, replica_groups=mesh['rep'=4,'fsdp'=8] {'fsdp'}, dimensions={0}, use_global_device_ids=true | all-gather | bytes 2304 | tf_op jit(solution)/shard_map/all_gather | solution.py:104
  51.4 18.7 %all-gather.3 = bf16[8,1,128]{2,1,0:T(2,128)(2,1)S(1)} all-gather(bf16[1,1,128]{2,1,0:T(2,128)(2,1)} %bitcast.203), channel_id=1, replica_groups=mesh['rep'=4,'fsdp'=8] {'fsdp'}, dimensions={0}, use_global_device_ids=true | all-gather | bytes 2304 | tf_op jit(solution)/shard_map/all_gather | solution.py:108
  70.7 17.5 %all-gather.4 = bf16[8,1,128]{2,1,0:T(2,128)(2,1)S(1)} all-gather(bf16[1,1,128]{2,1,0:T(2,128)(2,1)} %bitcast.204), channel_id=1, replica_groups=mesh['rep'=4,'fsdp'=8] {'fsdp'}, dimensions={0}, use_global_device_ids=true | all-gather | bytes 2304 | tf_op jit(solution)/shard_map/all_gather | solution.py:132
  88.8 18.7 %all-gather.5 = bf16[8,1,128]{2,1,0:T(2,128)(2,1)S(1)} all-gather(bf16[1,1,128]{2,1,0:T(2,128)(2,1)} %bitcast.205), channel_id=1, replica_groups=mesh['rep'=4,'fsdp'=8] {'fsdp'}, dimensions={0}, use_global_device_ids=true | all-gather | bytes 2304 | tf_op jit(solution)/shard_map/all_gather | solution.py:133
  109.0 16.5 %all-gather.6 = bf16[8,1,256]{2,1,0:T(2,128)(2,1)S(1)} all-gather(bf16[1,1,256]{2,1,0:T(2,128)(2,1)S(1)} %reshape.217), channel_id=1, replica_groups=mesh['rep'=4,'fsdp'=8] {'fsdp'}, dimensions={0}, use_global_device_ids=true | all-gather | bytes 4608 | tf_op jit(solution)/shard_map/all_gather | solution.py:135
  126.0 18.2 %all-gather.2 = bf16[8,1,256]{2,1,0:T(2,128)(2,1)S(1)} all-gather(bf16[1,1,256]{2,1,0:T(2,128)(2,1)S(1)} %reshape.209), channel_id=1, replica_groups=mesh['rep'=4,'fsdp'=8] {'fsdp'}, dimensions={0}, use_global_device_ids=true | all-gather | bytes 4608 | tf_op jit(solution)/shard_map/all_gather | solution.py:106
  144.3 7.4 fusion.67
  158.0 44.3 %while.26 = (s32[]{:T(128)}, bf16[8,768,128]{1,2,0:T(8,128)(2,1)}, f32[8,768]{1,0:T(8,128)}, s32[8,768]{1,0:T(8,128)}, bf16[8,768,128]{2,1,0:T(8,128)(2,1)}, /*i...) while((s32[]{:T(128)}, bf16[8,768,128]{1,2,0:T(8,128)(2,1)}, ...), condition=%wide.region_5.6_spmd, body=%wide.region_2.5_spmd.sunk | while | flops 308575488 | bytes 8705141 | solution.py:124
  202.3 4.7 fusion.81
  209.1 25.7 %all-gather.17.cloned.1.call-done = bf16[1024,2048]{1,0:T(8,128)(2,1)} async-done(((bf16[128,2048]{1,0:T(8,128)(2,1)}), bf16[1024,2048]{1,0:T(8,128)(2,1)}) %all-gather.17.cloned.1.call-update) | async-done | bytes 4194320 | tf_op jit(solution)/shard_map/all_gather | solution.py:134
  234.9 9.5 %fusion.72 = f32[768,2048]{1,0:T(8,128)} fusion(bf16[1024,2048]{1,0:T(8,128)(2,1)} %all-gather.17.cloned.1.call-done, f32[768,1024]{1,0:T(8,128)} %copy-done.2, f32[1024]{0:T(1024)S(1)} %bitcast.197, f32[1024]{0:T(1024)S(1)} %bitcast.186, f32[768]{0:T(1024)S(1)} %fusion.65, f32[768]{0:T(1024)S(1)} %broadcast_multiply_fusion), kind=kOutput, calls=%fused_computation.127 | convolution fusion | flops 3225157632 | bytes 13645824 | tf_op jit(solution)/shard_map/dot_general | solution.py:141
  244.4 63.9 %all-gather.19.cloned.1.call-done = bf16[2048,1024]{1,0:T(8,128)(2,1)} async-done(((bf16[256,1024]{1,0:T(8,128)(2,1)}), bf16[2048,1024]{1,0:T(8,128)(2,1)}) %all-gather.19.cloned.1.call-update) | async-done | bytes 4194320 | tf_op jit(solution)/shard_map/all_gather | solution.py:136
  308.3 11.2 %fusion.74 = (bf16[2048]{0:T(1024)(128)(2,1)}, bf16[768,2048]{1,0:T(8,128)(2,1)S(1)}) fusion(f32[768,2048]{1,0:T(8,128)} %fusion.72, f32[2048]{0:T(1024)S(1)} %bitcast.192, bf16[768,1024]{1,0:T(8,128)(2,1)S(1)} %copy-done.5, bf16[2048,1024]{1,0:T(8,128)(2,1)} %all-gather.19.cloned.1.call-done), kind=kOutput, calls=%fused_computation.129 | convolution fusion | flops 3255826432 | bytes 15216640 | tf_op jit(solution)/shard_map/dot_general | solution.py:77
  319.4 4.5 multiply_reduce_fusion.1
  328.0 3.1 convolution_convert_fusion.3
  331.2 8.6 %convolution_convert_fusion.2 = bf16[1024,2048]{1,0:T(8,128)(2,1)} fusion(bf16[768,2048]{1,0:T(8,128)(2,1)} %copy-done.33, f32[768,1024]{1,0:T(8,128)} %copy-done.2, f32[1024]{0:T(1024)S(1)} %bitcast.198, f32[1024]{0:T(1024)S(1)} %bitcast.189, f32[768]{0:T(1024)S(1)} %fusion.65, f32[768]{0:T(1024)S(1)} %broadcast_multiply_fusion), kind=kOutput, calls=%fused_computation.78 | convolution fusion | flops 3227254784 | bytes 10500096 | tf_op jit(solution)/shard_map/dot_general | solution.py:71
  340.1 3.9 fusion.63
  346.0 9.8 %convolution_convert_fusion.1 = bf16[2048,1024]{1,0:T(8,128)(2,1)} fusion(bf16[768,1024]{1,0:T(8,128)(2,1)S(1)} %copy-done.7, f32[768,2048]{1,0:T(8,128)} %fusion.72, f32[2048]{0:T(1024)S(1)} %bitcast.193), kind=kOutput, calls=%fused_computation.77 | convolution fusion | flops 3239051264 | bytes 12066816 | tf_op jit(solution)/shard_map/dot_general | solution.py:71
  356.1 103.2 %while.27 = (s32[]{:T(128)}, bf16[8,768,128]{1,2,0:T(8,128)(2,1)}, bf16[8,768,128]{1,2,0:T(8,128)(2,1)}, bf16[8,768,128]{1,2,0:T(8,128)(2,1)}, s32[8,768]{1,0:T(...) while((s32[]{:T(128)}, bf16[8,768,128]{1,2,0:T(8,128)(2,1)}, ...), condition=%wide.region_12.13_spmd, body=%wide.region_10.12_spmd.sunk | while | flops 762445056 | bytes 21464200 | solution.py:197
  361.3 2.2 fusion.131
  363.5 2.1 fusion.130
  374.2 2.2 fusion.131
  376.4 2.1 fusion.130
  387.1 2.2 fusion.131
  389.3 2.1 fusion.130
  400.0 2.2 fusion.131
  402.2 2.1 fusion.130
  412.9 2.2 fusion.131
  415.1 2.1 fusion.130
  425.8 2.2 fusion.131
  428.0 2.1 fusion.130
  438.7 2.2 fusion.131
  440.9 2.1 fusion.130
  451.6 2.2 fusion.131
  453.8 2.1 fusion.130
  459.3 11.1 %convolution_convert_fusion = bf16[1024,3072]{1,0:T(8,128)(2,1)} fusion(bf16[768,1024]{1,0:T(8,128)(2,1)} %param.19, f32[1024]{0:T(1024)} %bitcast.196, f32[1024]{0:T(1024)S(1)} %bitcast.182, f32[768]{0:T(1024)S(1)} %fusion.64, f32[768]{0:T(1024)S(1)} %broadcast_multiply_fusion.1, bf16[768,1024]{0,1:T(8,128)(2,1)} %bitcast.172, ...), kind=kOutput, calls=%fused_computation.66 | convolution fusion | flops 4853858304 | bytes 12597248 | tf_op jit(solution)/shard_map/dot_general | solution.py:71
  473.0 18.9 %all-gather.7 = bf16[8,1,128]{2,1,0:T(2,128)(2,1)S(1)} all-gather(bf16[1,1,128]{2,1,0:T(2,128)(2,1)S(1)} %bitcast.206), channel_id=1, replica_groups=mesh['rep'=4,'fsdp'=8] {'fsdp'}, dimensions={0}, use_global_device_ids=true | all-gather | bytes 2304 | tf_op jit(solution)/shard_map/all_gather | solution.py:137
  491.9 2.7 fusion.69
  497.0 9.4 %fusion.73 = (bf16[1024]{0:T(1024)(128)(2,1)S(1)}, f32[768]{0:T(1024)S(1)}, f32[768,1024]{1,0:T(8,128)S(1)}) fusion(f32[1024]{0:T(1024)S(1)} %bitcast.183, f32[768]{0:T(1024)S(1)} %broadcast_multiply_fusion.1, bf16[768,1024]{1,0:T(8,128)(2,1)S(1)} %copy-done.1, bf16[1024,3072]{1,0:T(8,128)(2,1)} %all-gather.13.cloned.1.call-done, ...), kind=kOutput, calls=%fused_computation.128 | convolution fusion | flops 4850710528 | bytes 15740928 | tf_op jit(solution)/shard_map/dot_general | solution.py:77
  508.2 34.6 %all-reduce.8 = (bf16[1024]{0:T(1024)(128)(2,1)S(1)}, bf16[1024]{0:T(1024)(128)(2,1)S(1)}, bf16[2048]{0:T(1024)(128)(2,1)S(1)}, bf16[1024]{0:T(1024)(128)(2,1)S(...) all-reduce(bf16[1024]{0:T(1024)(128)(2,1)S(1)} %get-tuple-element.1, ...), channel_id=2, replica_groups=mesh['rep'=4,'fsdp'=8] {'fsdp'}, use_global_device_ids=true, to_apply=%region_16.17.clone | all-reduce | flops 10240 | bytes 40960
  543.4 6.2 all-reduce.9
  553.8 4.5 add_convert_fusion
  558.3 23.1 %reduce-scatter.11.cloned.1.call-done = bf16[256,1024]{1,0:T(8,128)(2,1)} async-done(((bf16[2048,1024]{1,0:T(8,128)(2,1)}), bf16[256,1024]{1,0:T(8,128)(2,1)}) %reduce-scatter.11.cloned.1.call-update) | async-done | bytes 524304 | tf_op jit(solution)/shard_map/reduce_scatter | solution.py:181
  581.4 121.3 %reduce-scatter.5.cloned.1.call-done = bf16[128,3072]{1,0:T(8,128)(2,1)} async-done(((bf16[1024,3072]{1,0:T(8,128)(2,1)}), bf16[128,3072]{1,0:T(8,128)(2,1)}) %reduce-scatter.5.cloned.1.call-update) | async-done | bytes 786448 | tf_op jit(solution)/shard_map/reduce_scatter | solution.py:222
  702.8 10.3 %add_convert_fusion.1 = bf16[768,1024]{1,0:T(8,128)(2,1)} fusion(f32[768,1024]{1,0:T(8,128)} %copy-done.2, bf16[2048,1024]{1,0:T(8,128)(2,1)} %all-gather.19.cloned.1.call-done, f32[1024]{0:T(1024)S(1)} %bitcast.199, f32[768,2048]{1,0:T(8,128)} %fusion.72, f32[2048]{0:T(1024)S(1)} %bitcast.194), kind=kOutput, calls=%fused_computation.98 | convolution fusion | flops 3239313408 | bytes 15216640 | tf_op jit(solution)/shard_map/dot_general | solution.py:145
  713.0 42.9 %all-reduce.13.cloned.1.call-done = (bf16[128,3072]{1,0:T(8,128)(2,1)}, bf16[128,1024]{1,0:T(8,128)(2,1)}, bf16[128,2048]{1,0:T(8,128)(2,1)}, bf16[256,1024]{1,0:T(8,128)(2,1)}) async-done(((bf16[128,3072]{1,0:T(8,128)(2,1)}, bf16[128,1024]{1,0:T(8,128)(2,1)}, bf16[128,2048]{1,0:T(8,128)(2,1)}, bf16[256,1024]{1,0:T(8,128)(2,1)}), (bf16[128,3072]{1,0:T(8,128)(2,1)}, bf16[128,1024]{1,0:T(8,128)(2,1)}, ...) | async-done | bytes 2097168 | tf_op jit(solution)/shard_map/psum | solution.py:251
  757.9 2.4 convert_element_type.194
  (295 shorter events, 149.0 us)
Async XLA Ops:
  7.2 100.9 %copy-start = (bf16[768,1024]{1,0:T(8,128)(2,1)S(1)}, bf16[768,1024]{1,0:T(8,128)(2,1)}, u32[]{:S(2)}) copy-start(bf16[768,1024]{1,0:T(8,128)(2,1)} %param.19) | copy-start | bytes 4718596
  7.2 137.1 %all-gather.13.cloned.1.call-start = ((), (), s32[]{:S(2)}) async-start(), calls=%async_computation.4 | async-start | bytes 7077888 | tf_op jit(solution)/shard_map/all_gather | solution.py:105
  7.9 194.4 %all-gather.15.cloned.1.call-start = ((), (), s32[]{:S(2)}) async-start(), calls=%async_computation.5 | async-start | bytes 2359296 | tf_op jit(solution)/shard_map/all_gather | solution.py:107
  8.7 226.2 %all-gather.17.cloned.1.call-start = ((), (), s32[]{:S(2)}) async-start(), calls=%async_computation.6 | async-start | bytes 4718592 | tf_op jit(solution)/shard_map/all_gather | solution.py:134
  9.4 298.8 %all-gather.19.cloned.1.call-start = ((), (), s32[]{:S(2)}) async-start(), calls=%async_computation.7 | async-start | bytes 4718592 | tf_op jit(solution)/shard_map/all_gather | solution.py:136
  10.0 548.3 %reduce-scatter.7.cloned.1.call-start = ((), (), s32[]{:S(2)}) async-start(), calls=%async_computation.9 | async-start | bytes 2359296 | tf_op jit(solution)/shard_map/reduce_scatter | solution.py:228
  51.4 100.3 %copy-start.24 = (f32[8,1,128]{2,1,0:T(1,128)}, f32[8,1,128]{2,1,0:T(1,128)S(1)}, u32[]{:S(2)}) copy-start(f32[8,1,128]{2,1,0:T(1,128)S(1)} %convert_element_type.211) | copy-start | bytes 12292
  108.9 42.8 %copy-start.14 = (f32[768]{0:T(1024)}, f32[768]{0:T(1024)S(1)}, u32[]{:S(2)}) copy-start(f32[768]{0:T(1024)S(1)} %fusion.54) | copy-start | bytes 9220
  155.7 1.7 copy-start.22
  202.3 4.7 copy-start.8
  207.0 1.6 copy-start.2
  207.1 27.8 %copy-start.16 = (f32[8,1,128]{2,1,0:T(1,128)S(1)}, f32[8,1,128]{2,1,0:T(1,128)}, u32[]{:S(2)}) copy-start(f32[8,1,128]{2,1,0:T(1,128)} %convert_element_type.214) | copy-start | bytes 12292
  207.1 27.8 %copy-start.25 = (f32[8,1,128]{2,1,0:T(1,128)S(1)}, f32[8,1,128]{2,1,0:T(1,128)}, u32[]{:S(2)}) copy-start(f32[8,1,128]{2,1,0:T(1,128)} %convert_element_type.215) | copy-start | bytes 12292
  234.9 73.3 %copy-start.5 = (bf16[768,1024]{1,0:T(8,128)(2,1)S(1)}, bf16[768,1024]{1,0:T(8,128)(2,1)}, u32[]{:S(2)}) copy-start(bf16[768,1024]{1,0:T(8,128)(2,1)} %param.33) | copy-start | bytes 4718596
  234.9 73.3 %copy-start.20 = (f32[8,1,256]{2,1,0:T(1,128)S(1)}, f32[8,1,256]{2,1,0:T(1,128)}, u32[]{:S(2)}) copy-start(f32[8,1,256]{2,1,0:T(1,128)} %convert_element_type.216) | copy-start | bytes 24580
  308.2 11.2 %copy-start.3 = (f32[768,1024]{1,0:T(8,128)S(1)}, f32[768,1024]{1,0:T(8,128)}, u32[]{:S(2)}) copy-start(f32[768,1024]{1,0:T(8,128)} %copy-done.2) | copy-start | bytes 9437188
  308.2 11.2 %copy-start.30 = (bf16[1024,2048]{1,0:T(8,128)(2,1)S(1)}, bf16[1024,2048]{1,0:T(8,128)(2,1)}, u32[]{:S(2)}) copy-start(bf16[1024,2048]{1,0:T(8,128)(2,1)} %all-gather.17.cloned.1.call-done) | copy-start | bytes 12582916
  319.4 4.5 copy-start.33
  324.0 1.4 copy-start.6
  325.4 2.6 copy-start.31
  326.8 1.2 copy-start.11
  328.0 3.2 copy-start.17
  328.0 3.2 copy-start.26
  331.1 227.2 %reduce-scatter.9.cloned.1.call-start = ((), (), s32[]{:S(2)}) async-start(), calls=%async_computation.10 | async-start | bytes 4718592 | tf_op jit(solution)/shard_map/reduce_scatter | solution.py:175
  339.8 241.6 %reduce-scatter.11.cloned.1.call-start = ((), (), s32[]{:S(2)}) async-start(), calls=%async_computation.11 | async-start | bytes 4718592 | tf_op jit(solution)/shard_map/reduce_scatter | solution.py:181
  344.0 1.9 copy-start.7
  355.8 346.9 %reduce-scatter.5.cloned.1.call-start = ((), (), s32[]{:S(2)}) async-start(), calls=%async_computation.8 | async-start | bytes 7077888 | tf_op jit(solution)/shard_map/reduce_scatter | solution.py:222
  470.5 0.7 copy-start.32
  470.5 2.5 copy-start.29
  470.5 285.5 %all-reduce.13.cloned.1.call-start = ((), (), s32[]{:S(2)}) async-start(), calls=%async_computation.12 | async-start | bytes 4194304 | tf_op jit(solution)/shard_map/psum | solution.py:251
  494.6 1.4 copy-start.1
  494.6 1.9 copy-start.9
  494.6 2.3 copy-start.10
  497.0 9.4 %copy-start.15 = (f32[768]{0:T(1024)S(1)}, f32[768]{0:T(1024)}, u32[]{:S(2)}) copy-start(f32[768]{0:T(1024)} %copy-done.14) | copy-start | bytes 9220
  506.4 1.8 copy-start.4
  506.4 1.8 copy-start.18
  506.4 1.8 copy-start.19
  506.4 1.8 copy-start.23
  506.4 1.8 copy-start.27
  506.4 1.8 copy-start.28
  553.8 148.9 %copy-start.21 = (f32[8,1,256]{2,1,0:T(1,128)S(1)}, f32[8,1,256]{2,1,0:T(1,128)}, u32[]{:S(2)}) copy-start(f32[8,1,256]{2,1,0:T(1,128)} %convert_element_type.216) | copy-start | bytes 24580
  756.0 4.3 copy-start.13
  756.0 5.4 copy-start.12
Sparse Core Ops, SparseCore 0:
  10.2 101.6 all-gather.12
  114.0 47.2 all-gather.14
  163.5 71.3 all-gather.16
  236.9 71.3 all-gather.18
  331.2 66.9 reduce-scatter.6
  401.7 87.3 reduce-scatter.8
  492.8 88.6 reduce-scatter.10
  585.0 117.6 reduce-scatter.4
  705.3 50.6 all-reduce.12
where the time goes:
time: 782 us; the launch traced here: 769 us
  waiting for transfers between devices  280 us (36%)
  blocking collectives  189 us (24%)
  matrix products  183 us (23%)
  local copies, waits for them, and re-layouts  67.3 us (9%)
  other arithmetic  32.7 us (4%)
  between operations  15.8 us (2%)
    reduce_scatter x1, waiting for transfers between devices, on_device(): lax.psum_scatter(grad_joint.astype(jnp.bfloat16), 'fsdp', scatter_dimensi...  121 us
    all_gather x1, waiting for transfers between devices, on_device(): lax.all_gather(down_weight, 'fsdp', axis=0, tiled=True)  63.9 us
    psum x1, waiting for transfers between devices, on_device(): lax.psum(grad_joint.astype(jnp.bfloat16), 'rep').astype(jnp.float32)  42.9 us
    unnamed x1, blocking collectives  34.6 us
    dot_general x4, matrix products, transposed_dot(): lax.dot_general(left, right, (((0,), (0,)), ((), ())), preferred_element_...  32.7 us
    dot_general x4, matrix products, dot_transposed(): lax.dot_general(left, right, (((1,), (1,)), ((), ())), preferred_element_...  29 us
    dot_general x16, matrix products, block_scores(): lax.dot_general(queries, key_rows, (((1,), (1,)), ((), ())), preferred_el...  27.2 us
    all_gather x1, waiting for transfers between devices, on_device(): lax.all_gather(up_weight, 'fsdp', axis=0, tiled=True)  25.7 us
  transfers between devices with their start and end apart: 9, of which 5 were waited for; matrix products, arithmetic and copies ran while one was open for 32% of the time, Pallas kernels for 0%

commit v1 on v0

--- a/solution.py
+++ b/solution.py
@@ -248,7 +248,7 @@
     ) = (
         lax.psum(grad_gain_one.astype(jnp.bfloat16), "rep").astype(jnp.float32),
         lax.psum(grad_bias_one.astype(jnp.bfloat16), "rep").astype(jnp.float32),
-        lax.psum(grad_joint.astype(jnp.bfloat16), "rep").astype(jnp.float32),
+        jnp.sum(lax.all_gather(grad_joint.astype(jnp.bfloat16), "rep"), axis=0).astype(jnp.float32),
         lax.psum(grad_joint_shift.astype(jnp.bfloat16), "rep").astype(jnp.float32),
         lax.psum(grad_out.astype(jnp.bfloat16), "rep").astype(jnp.float32),
         lax.psum(grad_out_shift.astype(jnp.bfloat16), "rep").astype(jnp.float32),

time: 782 us -> 810 us (1.036)
  waiting for transfers between devices: 280 us -> 300 us
    reduce_scatter x1, waiting for transfers between devices: 23.1 us -> 91.6 us  [on_device(): lax.psum_scatter(grad_down.astype(jnp.bfloat16), 'fsdp', scatter_dimensio...]
    psum x1, waiting for transfers between devices: 42.9 us -> 0.01 us  [on_device(): lax.psum(grad_out.astype(jnp.bfloat16), 'rep').astype(jnp.float32)]
    reduce_scatter x1, waiting for transfers between devices: 121 us -> 99.2 us  [on_device(): lax.psum_scatter(grad_joint.astype(jnp.bfloat16), 'fsdp', scatter_dimensi...]
    reduce_scatter x1, waiting for transfers between devices: 0.01 us -> 18.4 us  [on_device(): lax.psum_scatter(grad_up.astype(jnp.bfloat16), 'fsdp', scatter_dimension=...]
  transfers between devices with their start and end apart: 9 -> 10, of which waited for: 5 -> 5; matrix products, arithmetic and copies ran while one was open for 32% -> 32% of each run, Pallas kernels for 0% -> 0%
where the time goes in v1:
time: 810 us; the launch traced here: 797 us
  waiting for transfers between devices  300 us (37%)
  blocking collectives  191 us (24%)
  matrix products  187 us (23%)
  local copies, waits for them, and re-layouts  66.3 us (8%)
  other arithmetic  35.9 us (4%)
  between operations  16.1 us (2%)
    reduce_scatter x1, waiting for transfers between devices, on_device(): lax.psum_scatter(grad_joint.astype(jnp.bfloat16), 'fsdp', scatter_dimensi...  99.2 us
    reduce_scatter x1, waiting for transfers between devices, on_device(): lax.psum_scatter(grad_down.astype(jnp.bfloat16), 'fsdp', scatter_dimensio...  91.6 us
    all_gather x1, waiting for transfers between devices, on_device(): lax.all_gather(down_weight, 'fsdp', axis=0, tiled=True)  65.6 us
    unnamed x1, blocking collectives  35.2 us
    dot_general x4, matrix products, transposed_dot(): lax.dot_general(left, right, (((0,), (0,)), ((), ())), preferred_element_...  32.7 us
    dot_general x4, matrix products, dot_transposed(): lax.dot_general(left, right, (((1,), (1,)), ((), ())), preferred_element_...  29 us
    dot_general x16, matrix products, block_scores(): lax.dot_general(queries, key_rows, (((1,), (1,)), ((), ())), preferred_el...  27.3 us
    all_gather x1, blocking collectives, on_device(): lax.all_gather(norm_gain, 'fsdp', axis=0, tiled=True)  22.8 us
  transfers between devices with their start and end apart: 10, of which 5 were waited for; matrix products, arithmetic and copies ran while one was open for 32% of the time, Pallas kernels for 0%

profile of v1, /device:TPU:0, one launch (start us, length us, event | category | flops | bytes accessed | tf_op | source)
XLA Modules:
  0.0 797.2 jit_solution(16214351803139515204)
XLA Ops:
  11.4 22.8 %all-gather.1 = bf16[8,1,128]{2,1,0:T(2,128)(2,1)S(1)} all-gather(bf16[1,1,128]{2,1,0:T(2,128)(2,1)} %bitcast.203), channel_id=1, replica_groups=mesh['rep'=4,'fsdp'=8] {'fsdp'}, dimensions={0}, use_global_device_ids=true | all-gather | bytes 2304 | tf_op jit(solution)/shard_map/all_gather | solution.py:103
  34.2 17.2 %all-gather.2 = bf16[8,1,128]{2,1,0:T(2,128)(2,1)S(1)} all-gather(bf16[1,1,128]{2,1,0:T(2,128)(2,1)} %bitcast.204), channel_id=1, replica_groups=mesh['rep'=4,'fsdp'=8] {'fsdp'}, dimensions={0}, use_global_device_ids=true | all-gather | bytes 2304 | tf_op jit(solution)/shard_map/all_gather | solution.py:104
  51.4 18.7 %all-gather.4 = bf16[8,1,128]{2,1,0:T(2,128)(2,1)S(1)} all-gather(bf16[1,1,128]{2,1,0:T(2,128)(2,1)} %bitcast.205), channel_id=1, replica_groups=mesh['rep'=4,'fsdp'=8] {'fsdp'}, dimensions={0}, use_global_device_ids=true | all-gather | bytes 2304 | tf_op jit(solution)/shard_map/all_gather | solution.py:108
  70.1 17.4 %all-gather.5 = bf16[8,1,128]{2,1,0:T(2,128)(2,1)S(1)} all-gather(bf16[1,1,128]{2,1,0:T(2,128)(2,1)} %bitcast.206), channel_id=1, replica_groups=mesh['rep'=4,'fsdp'=8] {'fsdp'}, dimensions={0}, use_global_device_ids=true | all-gather | bytes 2304 | tf_op jit(solution)/shard_map/all_gather | solution.py:132
  87.5 18.4 %all-gather.6 = bf16[8,1,128]{2,1,0:T(2,128)(2,1)S(1)} all-gather(bf16[1,1,128]{2,1,0:T(2,128)(2,1)} %bitcast.207), channel_id=1, replica_groups=mesh['rep'=4,'fsdp'=8] {'fsdp'}, dimensions={0}, use_global_device_ids=true | all-gather | bytes 2304 | tf_op jit(solution)/shard_map/all_gather | solution.py:133
  106.8 16.6 %all-gather.7 = bf16[8,1,256]{2,1,0:T(2,128)(2,1)S(1)} all-gather(bf16[1,1,256]{2,1,0:T(2,128)(2,1)S(1)} %reshape.218), channel_id=1, replica_groups=mesh['rep'=4,'fsdp'=8] {'fsdp'}, dimensions={0}, use_global_device_ids=true | all-gather | bytes 4608 | tf_op jit(solution)/shard_map/all_gather | solution.py:135
  123.4 18.2 %all-gather.3 = bf16[8,1,256]{2,1,0:T(2,128)(2,1)S(1)} all-gather(bf16[1,1,256]{2,1,0:T(2,128)(2,1)S(1)} %reshape.210), channel_id=1, replica_groups=mesh['rep'=4,'fsdp'=8] {'fsdp'}, dimensions={0}, use_global_device_ids=true | all-gather | bytes 4608 | tf_op jit(solution)/shard_map/all_gather | solution.py:106
  141.6 7.4 fusion.67
  153.0 2.3 copy_bitcast_fusion.1
  155.9 51.8 %while.26 = (s32[]{:T(128)}, bf16[8,768,128]{1,2,0:T(8,128)(2,1)}, f32[8,768]{1,0:T(8,128)}, s32[8,768]{1,0:T(8,128)}, bf16[8,768,128]{2,1,0:T(8,128)(2,1)}, /*i...) while((s32[]{:T(128)}, bf16[8,768,128]{1,2,0:T(8,128)(2,1)}, ...), condition=%wide.region_5.6_spmd, body=%wide.region_2.5_spmd.sunk | while | flops 308575488 | bytes 8703093 | solution.py:124
  207.7 4.5 fusion.81
  212.7 22.2 %all-gather.19.cloned.1.call-done = bf16[1024,2048]{1,0:T(8,128)(2,1)} async-done(((bf16[128,2048]{1,0:T(8,128)(2,1)}), bf16[1024,2048]{1,0:T(8,128)(2,1)}) %all-gather.19.cloned.1.call-update) | async-done | bytes 4194320 | tf_op jit(solution)/shard_map/all_gather | solution.py:134
  234.9 7.8 fusion.72
  242.7 65.6 %all-gather.21.cloned.1.call-done = bf16[2048,1024]{1,0:T(8,128)(2,1)} async-done(((bf16[256,1024]{1,0:T(8,128)(2,1)}), bf16[2048,1024]{1,0:T(8,128)(2,1)}) %all-gather.21.cloned.1.call-update) | async-done | bytes 4194320 | tf_op jit(solution)/shard_map/all_gather | solution.py:136
  308.2 11.3 %fusion.74 = (bf16[2048]{0:T(1024)(128)(2,1)}, bf16[768,2048]{1,0:T(8,128)(2,1)S(1)}) fusion(f32[768,2048]{1,0:T(8,128)} %fusion.72, f32[2048]{0:T(1024)S(1)} %bitcast.194, bf16[768,1024]{1,0:T(8,128)(2,1)} %param.33, bf16[2048,1024]{1,0:T(8,128)(2,1)} %all-gather.21.cloned.1.call-done), kind=kOutput, calls=%fused_computation.129 | convolution fusion | flops 3255826432 | bytes 15216640 | tf_op jit(solution)/shard_map/dot_general | solution.py:77
  319.5 4.5 multiply_reduce_fusion.1
  324.1 3.0 fusion.78
  329.7 3.1 convolution_convert_fusion.3
  333.1 8.6 %convolution_convert_fusion.2 = bf16[1024,2048]{1,0:T(8,128)(2,1)} fusion(bf16[768,2048]{1,0:T(8,128)(2,1)} %copy-done.26, f32[768,1024]{1,0:T(8,128)} %copy-done.2, f32[1024]{0:T(1024)S(1)} %bitcast.200, f32[1024]{0:T(1024)S(1)} %bitcast.191, f32[768]{0:T(1024)S(1)} %fusion.65, f32[768]{0:T(1024)S(1)} %broadcast_multiply_fusion), kind=kOutput, calls=%fused_computation.78 | convolution fusion | flops 3227254784 | bytes 10500096 | tf_op jit(solution)/shard_map/dot_general | solution.py:71
  341.8 3.9 fusion.63
  347.6 9.8 %convolution_convert_fusion.1 = bf16[2048,1024]{1,0:T(8,128)(2,1)} fusion(bf16[768,1024]{1,0:T(8,128)(2,1)S(1)} %copy-done.6, f32[768,2048]{1,0:T(8,128)} %fusion.72, f32[2048]{0:T(1024)S(1)} %bitcast.195), kind=kOutput, calls=%fused_computation.77 | convolution fusion | flops 3239051264 | bytes 12066816 | tf_op jit(solution)/shard_map/dot_general | solution.py:71
  357.8 103.2 %while.27 = (s32[]{:T(128)}, bf16[8,768,128]{1,2,0:T(8,128)(2,1)}, bf16[8,768,128]{1,2,0:T(8,128)(2,1)}, bf16[8,768,128]{1,2,0:T(8,128)(2,1)}, s32[8,768]{1,0:T(...) while((s32[]{:T(128)}, bf16[8,768,128]{1,2,0:T(8,128)(2,1)}, ...), condition=%wide.region_12.13_spmd, body=%wide.region_10.12_spmd.sunk | while | flops 762445056 | bytes 21464200 | solution.py:197
  363.0 2.2 fusion.131
  375.9 2.2 fusion.131
  378.1 2.1 fusion.130
  388.8 2.2 fusion.131
  390.9 2.1 fusion.130
  401.7 2.2 fusion.131
  403.9 2.1 fusion.130
  414.6 2.2 fusion.131
  416.7 2.1 fusion.130
  427.5 2.2 fusion.131
  440.4 2.2 fusion.131
  442.6 2.1 fusion.130
  453.3 2.2 fusion.131
  455.5 2.1 fusion.130
  461.0 11.1 %convolution_convert_fusion = bf16[1024,3072]{1,0:T(8,128)(2,1)} fusion(bf16[768,1024]{1,0:T(8,128)(2,1)} %param.19, f32[1024]{0:T(1024)} %bitcast.198, f32[1024]{0:T(1024)S(1)} %bitcast.184, f32[768]{0:T(1024)S(1)} %fusion.64, f32[768]{0:T(1024)S(1)} %broadcast_multiply_fusion.1, bf16[768,1024]{0,1:T(8,128)(2,1)} %bitcast.174, ...), kind=kOutput, calls=%fused_computation.66 | convolution fusion | flops 4853858304 | bytes 12597248 | tf_op jit(solution)/shard_map/dot_general | solution.py:71
  472.2 18.4 %reduce-scatter.9.cloned.1.call-done = bf16[128,2048]{1,0:T(8,128)(2,1)} async-done(((bf16[1024,2048]{1,0:T(8,128)(2,1)}), bf16[128,2048]{1,0:T(8,128)(2,1)}) %reduce-scatter.9.cloned.1.call-update) | async-done | bytes 524304 | tf_op jit(solution)/shard_map/reduce_scatter | solution.py:175
  490.7 91.6 %reduce-scatter.11.cloned.1.call-done = bf16[256,1024]{1,0:T(8,128)(2,1)} async-done(((bf16[2048,1024]{1,0:T(8,128)(2,1)}), bf16[256,1024]{1,0:T(8,128)(2,1)}) %reduce-scatter.11.cloned.1.call-update) | async-done | bytes 524304 | tf_op jit(solution)/shard_map/reduce_scatter | solution.py:181
  584.2 20.1 %all-gather.8 = bf16[8,1,128]{2,1,0:T(2,128)(2,1)S(1)} all-gather(bf16[1,1,128]{2,1,0:T(2,128)(2,1)S(1)} %bitcast.208), channel_id=1, replica_groups=mesh['rep'=4,'fsdp'=8] {'fsdp'}, dimensions={0}, use_global_device_ids=true | all-gather | bytes 2304 | tf_op jit(solution)/shard_map/all_gather | solution.py:137
  604.3 99.2 %reduce-scatter.5.cloned.1.call-done = bf16[128,3072]{1,0:T(8,128)(2,1)} async-done(((bf16[1024,3072]{1,0:T(8,128)(2,1)}), bf16[128,3072]{1,0:T(8,128)(2,1)}) %reduce-scatter.5.cloned.1.call-update) | async-done | bytes 786448 | tf_op jit(solution)/shard_map/reduce_scatter | solution.py:222
  703.6 2.7 fusion.69
  708.6 9.3 %fusion.73 = (bf16[1024]{0:T(1024)(128)(2,1)S(1)}, f32[768]{0:T(1024)S(1)}, f32[768,1024]{1,0:T(8,128)S(1)}) fusion(f32[1024]{0:T(1024)S(1)} %bitcast.185, f32[768]{0:T(1024)S(1)} %broadcast_multiply_fusion.1, bf16[768,1024]{1,0:T(8,128)(2,1)S(1)} %copy-done.1, bf16[1024,3072]{1,0:T(8,128)(2,1)} %all-gather.15.cloned.1.call-done, ...), kind=kOutput, calls=%fused_computation.128 | convolution fusion | flops 4850710528 | bytes 15740928 | tf_op jit(solution)/shard_map/dot_general | solution.py:77
  719.8 35.2 %all-reduce.8 = (bf16[1024]{0:T(1024)(128)(2,1)S(1)}, bf16[1024]{0:T(1024)(128)(2,1)S(1)}, bf16[2048]{0:T(1024)(128)(2,1)S(1)}, bf16[1024]{0:T(1024)(128)(2,1)S(...) all-reduce(bf16[1024]{0:T(1024)(128)(2,1)S(1)} %get-tuple-element.1, ...), channel_id=3, replica_groups=mesh['rep'=4,'fsdp'=8] {'fsdp'}, use_global_device_ids=true, to_apply=%region_16.17.clone | all-reduce | flops 10240 | bytes 40960
  755.6 6.6 all-reduce.9
  766.4 4.6 add_convert_fusion
  772.1 8.2 %add_convert_fusion.1 = bf16[768,1024]{1,0:T(8,128)(2,1)} fusion(f32[768,1024]{1,0:T(8,128)S(1)} %copy-done.3, bf16[2048,1024]{1,0:T(8,128)(2,1)S(1)} %copy-done.22, f32[1024]{0:T(1024)S(1)} %bitcast.201, f32[768,2048]{1,0:T(8,128)} %fusion.72, f32[2048]{0:T(1024)S(1)} %bitcast.196), kind=kOutput, calls=%fused_computation.98 | convolution fusion | flops 3239313408 | bytes 15216640 | tf_op jit(solution)/shard_map/dot_general | solution.py:145
  786.4 2.5 reduce_sum.214
  (285 shorter events, 157.5 us)
Async XLA Ops:
  7.2 98.8 %copy-start = (bf16[768,1024]{1,0:T(8,128)(2,1)S(1)}, bf16[768,1024]{1,0:T(8,128)(2,1)}, u32[]{:S(2)}) copy-start(bf16[768,1024]{1,0:T(8,128)(2,1)} %param.19) | copy-start | bytes 4718596
  7.2 134.4 %all-gather.15.cloned.1.call-start = ((), (), s32[]{:S(2)}) async-start(), calls=%async_computation.4 | async-start | bytes 7077888 | tf_op jit(solution)/shard_map/all_gather | solution.py:105
  7.9 199.8 %all-gather.17.cloned.1.call-start = ((), (), s32[]{:S(2)}) async-start(), calls=%async_computation.5 | async-start | bytes 2359296 | tf_op jit(solution)/shard_map/all_gather | solution.py:107
  8.7 226.2 %all-gather.19.cloned.1.call-start = ((), (), s32[]{:S(2)}) async-start(), calls=%async_computation.6 | async-start | bytes 4718592 | tf_op jit(solution)/shard_map/all_gather | solution.py:134
  9.4 298.8 %all-gather.21.cloned.1.call-start = ((), (), s32[]{:S(2)}) async-start(), calls=%async_computation.7 | async-start | bytes 4718592 | tf_op jit(solution)/shard_map/all_gather | solution.py:136
  10.0 462.2 %reduce-scatter.7.cloned.1.call-start = ((), (), s32[]{:S(2)}) async-start(), calls=%async_computation.9 | async-start | bytes 2359296 | tf_op jit(solution)/shard_map/reduce_scatter | solution.py:228
  51.4 97.6 %copy-start.18 = (f32[8,1,128]{2,1,0:T(1,128)}, f32[8,1,128]{2,1,0:T(1,128)S(1)}, u32[]{:S(2)}) copy-start(f32[8,1,128]{2,1,0:T(1,128)S(1)} %convert_element_type.213) | copy-start | bytes 12292
  106.8 42.2 %copy-start.10 = (f32[768]{0:T(1024)}, f32[768]{0:T(1024)S(1)}, u32[]{:S(2)}) copy-start(f32[768]{0:T(1024)S(1)} %fusion.54) | copy-start | bytes 9220
  123.4 224.3 %copy-start.14 = (f32[8,1,256]{2,1,0:T(1,128)}, f32[8,1,256]{2,1,0:T(1,128)S(1)}, u32[]{:S(2)}) copy-start(f32[8,1,256]{2,1,0:T(1,128)S(1)} %convert_element_type.218) | copy-start | bytes 24580
  153.0 2.3 copy-start.16
  212.3 107.2 %copy-start.2 = (f32[768,1024]{1,0:T(8,128)}, f32[768,1024]{1,0:T(8,128)S(1)}, u32[]{:S(2)}) copy-start(f32[768,1024]{1,0:T(8,128)S(1)} %get-tuple-element.191) | copy-start | bytes 9437188
  308.2 11.3 %copy-start.23 = (bf16[1024,2048]{1,0:T(8,128)(2,1)S(1)}, bf16[1024,2048]{1,0:T(8,128)(2,1)}, u32[]{:S(2)}) copy-start(bf16[1024,2048]{1,0:T(8,128)(2,1)} %all-gather.19.cloned.1.call-done) | copy-start | bytes 12582916
  319.5 4.5 copy-start.26
  324.1 3.0 copy-start.5
  327.1 2.6 copy-start.24
  328.5 1.2 copy-start.9
  332.8 157.8 %reduce-scatter.9.cloned.1.call-start = ((), (), s32[]{:S(2)}) async-start(), calls=%async_computation.10 | async-start | bytes 4718592 | tf_op jit(solution)/shard_map/reduce_scatter | solution.py:175
  341.7 240.5 %reduce-scatter.11.cloned.1.call-start = ((), (), s32[]{:S(2)}) async-start(), calls=%async_computation.11 | async-start | bytes 4718592 | tf_op jit(solution)/shard_map/reduce_scatter | solution.py:181
  345.7 1.9 copy-start.6
  357.5 346.1 %reduce-scatter.5.cloned.1.call-start = ((), (), s32[]{:S(2)}) async-start(), calls=%async_computation.8 | async-start | bytes 7077888 | tf_op jit(solution)/shard_map/reduce_scatter | solution.py:222
  472.1 110.2 %copy-start.25 = (u32[32]{0:T(128)S(1)}, u32[32]{0:T(128)}, u32[]{:S(2)}) copy-start(u32[32]{0:T(128)} %constant.86) | copy-start | bytes 388
  472.1 112.1 %copy-start.21 = (bf16[128]{0:T(256)(128)(2,1)S(1)}, bf16[128]{0:T(256)(128)(2,1)}, u32[]{:S(2)}) copy-start(bf16[128]{0:T(256)(128)(2,1)} %param.32) | copy-start | bytes 772
  472.2 308.2 %all-reduce.13.cloned.1.call-start = ((), (), s32[]{:S(2)}) async-start(), calls=%async_computation.13 | async-start | bytes 2621440 | tf_op jit(solution)/shard_map/psum | solution.py:253
  582.3 204.1 %all-gather.23.cloned.1.call-start = ((), (), s32[]{:S(2)}) async-start(), calls=%async_computation.12 | async-start | bytes 3932160 | tf_op jit(solution)/shard_map/all_gather | solution.py:251
  706.3 1.4 copy-start.1
  706.3 1.9 copy-start.7
  706.3 2.3 copy-start.8
  708.6 9.3 %copy-start.11 = (f32[768]{0:T(1024)S(1)}, f32[768]{0:T(1024)}, u32[]{:S(2)}) copy-start(f32[768]{0:T(1024)} %copy-done.10) | copy-start | bytes 9220
  717.9 1.8 copy-start.4
  717.9 1.8 copy-start.12
  717.9 1.8 copy-start.13
  717.9 1.8 copy-start.17
  717.9 1.8 copy-start.19
  717.9 1.8 copy-start.20
  766.4 4.7 copy-start.3
  766.4 4.7 copy-start.15
  766.4 5.7 copy-start.22
Sparse Core Ops, SparseCore 0:
  10.2 101.6 all-gather.14
  114.0 47.2 all-gather.16
  163.5 71.3 all-gather.18
  236.9 71.3 all-gather.20
  332.9 66.8 reduce-scatter.6
  403.3 87.3 reduce-scatter.8
  494.3 87.9 reduce-scatter.10
  585.8 117.6 reduce-scatter.4
  706.1 38.4 all-reduce.12
  746.0 28.6 all-gather.22
